TPU v7x, 32 devices: a whole 2x2x4 slice. The times are simulated.
32 devices in a mesh: rep: 4 (over y, x), seq: 8 (over z, core).
Axes of the slice: x: 2, y: 2, z: 4, core: 2. Of those that a mesh axis runs over, the one named last changes fastest.
Arguments:
- inputs: bfloat16 [4, 2048, 1536], P('rep', 'seq'), may hold values from -13 to 13
- segment_ids: int32 [4, 2048], P('rep'), may hold values from 0 to 7, as said below
- valid_mask: int32 [4, 2048], P('rep'), may hold values from 0 to 1, as said below
- input_weight: bfloat16 [1536, 4608], P('seq'), may hold values from -0.15625 to 0.15625
- output_weight: bfloat16 [1536, 1536], P('seq'), may hold values from -0.15625 to 0.15625
- conv_kernel: float32 [16, 6, 11], replicated, may hold values from -1.2 to 1.2
- head_mix: float32 [8, 2, 2], replicated, may hold values from 0.2 to 1
- first_gain: float32 [1536], replicated, may hold values from 0.5 to 1.5
- second_gain: float32 [1536], replicated, may hold values from 0.5 to 1.5
- group_gain: float32 [1536], replicated, may hold values from 0.5 to 1.5
- gate_weight: bfloat16 [1536, 4096], P(None, 'seq'), may hold values from -0.15625 to 0.15625
- up_weight: bfloat16 [1536, 4096], P(None, 'seq'), may hold values from -0.15625 to 0.15625
- down_weight: bfloat16 [4096, 1536], P('seq'), may hold values from -0.09375 to 0.09375
- cotangent: bfloat16 [4, 2048, 1536], P('rep', 'seq'), may hold values from -17 to 17
Outputs:
- output: bfloat16 [4, 2048, 1536], P('rep', 'seq')
- grad_inputs: bfloat16 [4, 2048, 1536], P('rep', 'seq')
- grad_input_weight: float32 [1536, 4608], P('seq')
- grad_output_weight: float32 [1536, 1536], P('seq')
- grad_kernel: float32 [16, 6, 11], replicated
- grad_mix: float32 [8, 2, 2], replicated
- grad_first_gain: float32 [1536], replicated
- grad_second_gain: float32 [1536], replicated
- grad_group_gain: float32 [1536], replicated
- grad_gate: float32 [1536, 4096], P(None, 'seq')
- grad_up: float32 [1536, 4096], P(None, 'seq')
- grad_down: float32 [4096, 1536], P('seq')
Inputs may be any that keep to these rules, and one draw needn't show every extreme that they name: `segment_ids`: segment ids never fall along a sequence and start at 0. The positions k * 1024 to (k + 1) * 1024 - 1 form frame k; every document lies inside one frame, a frame holds one to four documents, the first frame of the first sequence is a single document of exactly 1024 positions, and every frame of the last sequence holds four documents. `valid_mask`: in each frame the positions with 0 form its tail, at most 256 of them; the first frame of the first sequence has none.
All inputs are finite; a program needn't handle non-finite values.
Results may differ from a plain program's by a relative error of at most 0.02.
Values may be sent and summed in bfloat16 or wider, within the bound.
A program may use at most 384 MiB of HBM per device.

v0:
```python
import jax
import jax.numpy as jnp
from jax import lax
from jax.sharding import PartitionSpec as P

REACH = 4
EPS = 1e-06
HIGHEST = lax.Precision.HIGHEST


def from_behind(x, axis, by):
    count = lax.axis_size(axis)
    pairs = [(i, i + by) for i in range(count) if 0 <= i + by < count]
    return lax.ppermute(x, axis, pairs)


def convolve(logits, kernel, rows, columns):
    rim_rows = kernel.shape[1] - 1
    key_span = kernel.shape[2] - 1
    result = jnp.zeros((logits.shape[0], rows, columns), jnp.float32)
    for row_tap in range(kernel.shape[1]):
        for col_tap in range(kernel.shape[2]):
            weight = kernel[:, row_tap, col_tap][:, None, None]
            result = (
                result
                + weight
                * logits[
                    :,
                    rim_rows - row_tap : rim_rows - row_tap + rows,
                    key_span - col_tap : key_span - col_tap + columns,
                ]
            )
    return result


def convolve_back(grads, kernel):
    rim_rows = kernel.shape[1] - 1
    key_span = kernel.shape[2] - 1
    rows = grads.shape[1] + rim_rows
    columns = grads.shape[2] + key_span
    padded = jnp.pad(grads, ((0, 0), (rim_rows, rim_rows), (key_span, key_span)))
    result = jnp.zeros((grads.shape[0], rows, columns), jnp.float32)
    for row_tap in range(kernel.shape[1]):
        for col_tap in range(kernel.shape[2]):
            weight = kernel[:, row_tap, col_tap][:, None, None]
            result = (
                result + weight * padded[:, row_tap : row_tap + rows, col_tap : col_tap + columns]
            )
    return result


def kernel_grads(grads, logits, taps_rows, taps_cols):
    rim_rows = taps_rows - 1
    key_span = taps_cols - 1
    rows = grads.shape[1]
    columns = grads.shape[2]
    entries = []
    for row_tap in range(taps_rows):
        line_sums = []
        for col_tap in range(taps_cols):
            window_part = logits[
                :,
                rim_rows - row_tap : rim_rows - row_tap + rows,
                key_span - col_tap : key_span - col_tap + columns,
            ]
            line_sums.append(jnp.sum(grads * window_part, axis=(1, 2)))
        entries.append(jnp.stack(line_sums, axis=-1))
    return jnp.stack(entries, axis=1)


def attend_group(operands, mask_ext, mask_own, row_valid, score_scale):
    query_g, key_g, value_g, kernel_g, mixing_g = operands
    rows = mask_own.shape[0]
    columns = mask_own.shape[1]
    raw = jnp.einsum("qhd,khd->hqk", query_g, key_g, preferred_element_type=jnp.float32)
    logits = raw * score_scale * mask_ext
    conv = convolve(logits, kernel_g, rows, columns)
    allowed = mask_own > 0
    peak = jnp.max(jnp.where(allowed, conv, -1e30), axis=-1, keepdims=True)
    peak = jnp.where(row_valid > 0, peak, 0.0)
    expo = jnp.where(allowed, jnp.exp(conv - peak), 0.0)
    denom = jnp.sum(expo, axis=-1, keepdims=True) + 1.0 - row_valid
    prob = expo / denom
    mixed = (
        mixing_g[:, 0][:, None, None] * prob[0][None]
        + mixing_g[:, 1][:, None, None] * prob[1][None]
    )
    mixed_low = mixed.astype(jnp.bfloat16)
    result = jnp.einsum("hqk,khd->qhd", mixed_low, value_g, preferred_element_type=jnp.float32)
    return (result, peak + jnp.log(denom))


def attend_group_back(operands, mask_ext, mask_own, score_scale):
    query_g, key_g, value_g, kernel_g, mixing_g, dresult_g, lse_g = operands
    rows = mask_own.shape[0]
    columns = mask_own.shape[1]
    raw = jnp.einsum("qhd,khd->hqk", query_g, key_g, preferred_element_type=jnp.float32)
    logits = raw * score_scale * mask_ext
    conv = convolve(logits, kernel_g, rows, columns)
    allowed = mask_own > 0
    prob = jnp.where(allowed, jnp.exp(conv - lse_g), 0.0)
    mixed = (
        mixing_g[:, 0][:, None, None] * prob[0][None]
        + mixing_g[:, 1][:, None, None] * prob[1][None]
    )
    mixed_low = mixed.astype(jnp.bfloat16)
    dmixed = jnp.einsum("qhd,khd->hqk", dresult_g, value_g, preferred_element_type=jnp.float32)
    dvalue = jnp.einsum("hqk,qhd->khd", mixed_low, dresult_g, preferred_element_type=jnp.float32)
    dmixing = jnp.stack(
        [
            jnp.sum(dmixed * prob[0][None], axis=(1, 2)),
            jnp.sum(dmixed * prob[1][None], axis=(1, 2)),
        ],
        axis=-1,
    )
    dprob = (
        mixing_g[0][:, None, None] * dmixed[0][None] + mixing_g[1][:, None, None] * dmixed[1][None]
    )
    dconv = prob * (dprob - jnp.sum(prob * dprob, axis=-1, keepdims=True))
    dkernel = kernel_grads(dconv, logits, kernel_g.shape[1], kernel_g.shape[2])
    dlogits = convolve_back(dconv, kernel_g) * mask_ext * score_scale
    dquery = jnp.einsum(
        "hqk,khd->qhd",
        dlogits,
        key_g.astype(jnp.float32),
        precision=HIGHEST,
        preferred_element_type=jnp.float32,
    )
    dkey = jnp.einsum(
        "hqk,qhd->khd",
        dlogits,
        query_g.astype(jnp.float32),
        precision=HIGHEST,
        preferred_element_type=jnp.float32,
    )
    return (dquery, dkey, dvalue, dkernel, dmixing)


def rms_scale(values):
    return lax.rsqrt(jnp.mean(values * values, axis=-1, keepdims=True) + EPS)


def norm_back(grad_out, values, inv_scale, gain):
    scaled_grad = grad_out * gain
    inner = jnp.mean(scaled_grad * values, axis=-1, keepdims=True)
    return inv_scale * scaled_grad - values * inv_scale**3 * inner


def on_device(
    inputs,
    segment_ids,
    valid_mask,
    input_weight,
    output_weight,
    conv_kernel,
    head_mix,
    first_gain,
    second_gain,
    group_gain,
    gate_weight,
    up_weight,
    down_weight,
    cotangent,
):
    tokens = inputs.shape[1]
    model_width = inputs.shape[2]
    head_count = conv_kernel.shape[0]
    head_dim = model_width // head_count
    groups = head_mix.shape[0]
    rim_rows = conv_kernel.shape[1] - 1
    half_span = conv_kernel.shape[2] // 2
    window = REACH * tokens
    score_scale = head_dim ** (-0.5)
    seq_rank = lax.axis_index("seq")
    row_start = seq_rank * tokens
    window_start = row_start - (REACH - 1) * tokens
    resid_in = inputs[0].astype(jnp.float32)
    grad_out = cotangent[0].astype(jnp.float32)
    offset = window + half_span
    segment_pad = jnp.concatenate(
        [jnp.full((offset,), -1, jnp.int32), segment_ids[0], jnp.full((half_span,), -1, jnp.int32)]
    )
    valid_pad = jnp.concatenate(
        [jnp.zeros((offset,), jnp.int32), valid_mask[0], jnp.zeros((half_span,), jnp.int32)]
    )
    query_pos = row_start - rim_rows + jnp.arange(tokens + rim_rows, dtype=jnp.int32)
    key_pos = window_start - half_span + jnp.arange(window + 2 * half_span, dtype=jnp.int32)
    query_seg = lax.dynamic_slice_in_dim(
        segment_pad, row_start - rim_rows + offset, tokens + rim_rows
    )
    key_seg = lax.dynamic_slice_in_dim(
        segment_pad, window_start - half_span + offset, window + 2 * half_span
    )
    query_live = lax.dynamic_slice_in_dim(
        valid_pad, row_start - rim_rows + offset, tokens + rim_rows
    )
    key_live = lax.dynamic_slice_in_dim(
        valid_pad, window_start - half_span + offset, window + 2 * half_span
    )
    mask_ext = (
        (query_seg[:, None] == key_seg[None, :])
        & (key_pos[None, :] <= query_pos[:, None])
        & (query_live[:, None] > 0)
        & (key_live[None, :] > 0)
    ).astype(jnp.float32)
    mask_own = mask_ext[rim_rows:, half_span : half_span + window]
    row_valid = query_live[rim_rows:].astype(jnp.float32)[:, None]
    full_input, full_output = (
        lax.all_gather(input_weight, "seq", axis=0, tiled=True),
        lax.all_gather(output_weight, "seq", axis=0, tiled=True),
    )
    first_scale = rms_scale(resid_in)
    normed_in = (resid_in * first_scale * first_gain).astype(jnp.bfloat16)
    projected = jnp.dot(normed_in, full_input, preferred_element_type=jnp.float32).astype(
        jnp.bfloat16
    )
    query = projected[:, :model_width]
    keys_values = projected[:, model_width:]
    query_rim = from_behind(query[tokens - rim_rows :], "seq", 1)
    query_ext = jnp.concatenate([query_rim, query], axis=0)
    pieces = [keys_values]
    for distance in range(1, REACH):
        pieces.append(from_behind(keys_values, "seq", distance))
    window_rows = jnp.concatenate(pieces[::-1], axis=0)
    key_ext = jnp.pad(window_rows[:, :model_width], ((half_span, half_span), (0, 0)))
    value_window = window_rows[:, model_width:]

    def split_heads(values):
        return values.reshape(values.shape[0], groups, 2, head_dim).transpose(1, 0, 2, 3)

    def merge_heads(values):
        return values.transpose(1, 0, 2, 3).reshape(values.shape[1], model_width)

    query_groups = split_heads(query_ext)
    key_groups = split_heads(key_ext)
    value_groups = split_heads(value_window)
    kernel_groups = conv_kernel.reshape(groups, 2, conv_kernel.shape[1], conv_kernel.shape[2])
    result_groups, lse_groups = lax.map(
        lambda operands: attend_group(operands, mask_ext, mask_own, row_valid, score_scale),
        (query_groups, key_groups, value_groups, kernel_groups, head_mix),
    )
    attended = merge_heads(result_groups)
    shaped = attended.reshape(tokens, head_count, head_dim)
    centred = shaped - jnp.mean(shaped, axis=-1, keepdims=True)
    inv_std = lax.rsqrt(jnp.mean(centred * centred, axis=-1, keepdims=True) + EPS)
    unit_heads = centred * inv_std
    unit = unit_heads.reshape(tokens, model_width)
    normed = (unit * group_gain).astype(jnp.bfloat16)
    branch = jnp.dot(normed, full_output, preferred_element_type=jnp.float32)
    resid = resid_in + row_valid * branch
    second_scale = rms_scale(resid)
    normed_mid = (resid * second_scale * second_gain).astype(jnp.bfloat16)
    dmlp = (row_valid * grad_out).astype(jnp.bfloat16)
    contract_rows = (((0,), (0,)), ((), ()))
    inputs_all = lax.all_gather(normed_mid, "seq", axis=0, tiled=True)
    gate = jnp.dot(inputs_all, gate_weight, preferred_element_type=jnp.float32)
    up_proj = jnp.dot(inputs_all, up_weight, preferred_element_type=jnp.float32)
    hidden = (jax.nn.silu(gate) * up_proj).astype(jnp.bfloat16)
    mlp = lax.psum_scatter(
        jnp.dot(hidden, down_weight, preferred_element_type=jnp.float32).astype(jnp.bfloat16),
        "seq",
        scatter_dimension=0,
        tiled=True,
    ).astype(jnp.float32)
    result = resid + row_valid * mlp
    dmlp_all = lax.all_gather(dmlp, "seq", axis=0, tiled=True)
    dhidden = jnp.dot(dmlp_all, down_weight.T, preferred_element_type=jnp.float32)
    sigmoid_gate = jax.nn.sigmoid(gate)
    gate_grad = (dhidden * up_proj * sigmoid_gate * (1.0 + gate * (1.0 - sigmoid_gate))).astype(
        jnp.bfloat16
    )
    up_grad = (dhidden * gate * sigmoid_gate).astype(jnp.bfloat16)
    grad_down = lax.dot_general(hidden, dmlp_all, contract_rows, preferred_element_type=jnp.float32)
    grad_gate = lax.dot_general(
        inputs_all, gate_grad, contract_rows, preferred_element_type=jnp.float32
    )
    grad_up = lax.dot_general(
        inputs_all, up_grad, contract_rows, preferred_element_type=jnp.float32
    )
    dmid = lax.psum_scatter(
        (
            jnp.dot(gate_grad, gate_weight.T, preferred_element_type=jnp.float32)
            + jnp.dot(up_grad, up_weight.T, preferred_element_type=jnp.float32)
        ).astype(jnp.bfloat16),
        "seq",
        scatter_dimension=0,
        tiled=True,
    ).astype(jnp.float32)
    second_part = jnp.sum(dmid * resid * second_scale, axis=0)
    dresid = grad_out + norm_back(dmid, resid, second_scale, second_gain)
    dbranch = (row_valid * dresid).astype(jnp.bfloat16)
    whole_output_grad = lax.dot_general(
        normed, dbranch, contract_rows, preferred_element_type=jnp.float32
    )
    dnormed = jnp.dot(dbranch, full_output.T, preferred_element_type=jnp.float32)
    group_part = jnp.sum(dnormed * unit, axis=0)
    dunit = (dnormed * group_gain).reshape(tokens, head_count, head_dim)
    dshaped = inv_std * (
        dunit
        - jnp.mean(dunit, axis=-1, keepdims=True)
        - unit_heads * jnp.mean(dunit * unit_heads, axis=-1, keepdims=True)
    )
    dattended = dshaped.reshape(tokens, model_width).astype(jnp.bfloat16)
    dquery_g, dkey_g, dvalue_g, dkernel_g, dmixing = lax.map(
        lambda operands: attend_group_back(operands, mask_ext, mask_own, score_scale),
        (
            query_groups,
            key_groups,
            value_groups,
            kernel_groups,
            head_mix,
            split_heads(dattended),
            lse_groups,
        ),
    )
    dquery_ext = merge_heads(dquery_g)
    dkey_window = merge_heads(dkey_g)[half_span : half_span + window]
    dvalue_window = merge_heads(dvalue_g)
    dpair_window = jnp.concatenate([dkey_window, dvalue_window], axis=1)
    dpair = dpair_window[(REACH - 1) * tokens :]
    for distance in range(1, REACH):
        block_first = (REACH - 1 - distance) * tokens
        dpair = dpair + from_behind(
            dpair_window[block_first : block_first + tokens].astype(jnp.bfloat16), "seq", -distance
        ).astype(jnp.float32)
    rim_grad = from_behind(dquery_ext[:rim_rows], "seq", -1)
    dquery_own = dquery_ext[rim_rows:]
    dquery_own = jnp.concatenate(
        [dquery_own[: tokens - rim_rows], dquery_own[tokens - rim_rows :] + rim_grad], axis=0
    )
    dprojected = jnp.concatenate([dquery_own, dpair], axis=1).astype(jnp.bfloat16)
    whole_input_grad = lax.dot_general(
        normed_in, dprojected, contract_rows, preferred_element_type=jnp.float32
    )
    dnormin = jnp.dot(dprojected, full_input.T, preferred_element_type=jnp.float32)
    first_part = jnp.sum(dnormin * resid_in * first_scale, axis=0)
    grad_in = dresid + norm_back(dnormin, resid_in, first_scale, first_gain)
    input_shard, output_shard = (
        lax.psum_scatter(
            whole_input_grad.astype(jnp.bfloat16), "seq", scatter_dimension=0, tiled=True
        ).astype(jnp.float32),
        lax.psum_scatter(
            whole_output_grad.astype(jnp.bfloat16), "seq", scatter_dimension=0, tiled=True
        ).astype(jnp.float32),
    )
    kernel_part = dkernel_g.reshape(head_count, conv_kernel.shape[1], conv_kernel.shape[2])
    grad_kernel, grad_mix, grad_first, grad_second, grad_group = lax.psum(
        (kernel_part, dmixing, first_part, second_part, group_part), ("rep", "seq")
    )
    grad_input_w, grad_output_w, grad_gate, grad_up, grad_down = (
        lax.psum(input_shard.astype(jnp.bfloat16), "rep").astype(jnp.float32),
        lax.psum(output_shard.astype(jnp.bfloat16), "rep").astype(jnp.float32),
        lax.psum(grad_gate.astype(jnp.bfloat16), "rep").astype(jnp.float32),
        lax.psum(grad_up.astype(jnp.bfloat16), "rep").astype(jnp.float32),
        lax.psum(grad_down.astype(jnp.bfloat16), "rep").astype(jnp.float32),
    )
    return (
        result.astype(jnp.bfloat16)[None],
        grad_in.astype(jnp.bfloat16)[None],
        grad_input_w,
        grad_output_w,
        grad_kernel,
        grad_mix,
        grad_first,
        grad_second,
        grad_group,
        grad_gate,
        grad_up,
        grad_down,
    )


def solution(mesh):
    in_specs = (
        P("rep", "seq", None),
        P("rep", None),
        P("rep", None),
        P("seq", None),
        P("seq", None),
        P(),
        P(),
        P(),
        P(),
        P(),
        P(None, "seq"),
        P(None, "seq"),
        P("seq", None),
        P("rep", "seq", None),
    )
    out_specs = (
        P("rep", "seq", None),
        P("rep", "seq", None),
        P("seq", None),
        P("seq", None),
        P(),
        P(),
        P(),
        P(),
        P(),
        P(None, "seq"),
        P(None, "seq"),
        P("seq", None),
    )
    return jax.shard_map(
        on_device, mesh=mesh, in_specs=in_specs, out_specs=out_specs, check_vma=False
    )
```

profile of v0, /device:TPU:0, one launch (start us, length us, event | category | flops | bytes accessed | tf_op | source)
XLA Modules:
  0.0 4016.5 jit_solution(8021908718773649853)
XLA Ops:
  9.3 132.8 %all-gather.5.cloned.1.call-done = bf16[1536,4608]{1,0:T(8,128)(2,1)} async-done(((bf16[192,4608]{1,0:T(8,128)(2,1)}), bf16[1536,4608]{1,0:T(8,128)(2,1)}) %all-gather.5.cloned.1.call-update) | async-done | bytes 14155792 | tf_op jit(solution)/shard_map/all_gather | solution.py:209
  178.6 39.8 collective-permute-done.1
  218.4 47.0 %collective-permute-done = bf16[256,3072]{1,0:T(8,128)(2,1)} collective-permute-done((bf16[256,3072]{1,0:T(8,128)(2,1)}, bf16[256,3072]{1,0:T(8,128)(2,1)}, u32[]{:S(2)}, u32[]{:S(2)}) %collective-permute-start) | collective-permute-done | bytes 1572896 | tf_op jit(solution)/shard_map/ppermute | solution.py:14
  286.9 341.3 %while.34 = (s32[]{:T(128)}, f32[8,256,2,96]{1,3,2,0:T(8,128)S(1)}, f32[8,2,256,1]{2,1,3,0:T(2,128)}, bf16[8,1024,2,96]{1,3,2,0:T(8,128)(2,1)}, f32[8,2,2]{2,1,0...) while((s32[]{:T(128)}, f32[8,256,2,96]{1,3,2,0:T(8,128)S(1)}, ...), condition=%wide.region_4.5_spmd.clone, body=%wide.region_1.4_spmd.clone.sunk | while | flops 281692032 | bytes 160720624 | solution.py:238
  291.5 34.6 select_reduce_fusion.2
  334.2 34.6 select_reduce_fusion.2
  376.8 34.6 select_reduce_fusion.2
  419.5 34.6 select_reduce_fusion.2
  462.1 34.6 select_reduce_fusion.2
  504.7 34.6 select_reduce_fusion.2
  547.4 34.6 select_reduce_fusion.2
  590.0 34.6 select_reduce_fusion.2
  652.1 102.0 %all-gather.9.cloned.1.call-done = bf16[2048,1536]{1,0:T(8,128)(2,1)} async-done(((bf16[256,1536]{1,0:T(8,128)(2,1)}), bf16[2048,1536]{1,0:T(8,128)(2,1)}) %all-gather.9.cloned.1.call-update) | async-done | bytes 6291472 | tf_op jit(solution)/shard_map/all_gather | solution.py:255
  767.9 51.8 %all-gather.11.cloned.1.call-done = bf16[2048,1536]{1,0:T(8,128)(2,1)} async-done(((bf16[256,1536]{1,0:T(8,128)(2,1)}), bf16[2048,1536]{1,0:T(8,128)(2,1)}) %all-gather.11.cloned.1.call-update) | async-done | bytes 6291472 | tf_op jit(solution)/shard_map/all_gather | solution.py:266
  848.9 61.1 %reduce-scatter.7.cloned.1.call-done = bf16[256,1536]{1,0:T(8,128)(2,1)} async-done(((bf16[2048,1536]{1,0:T(8,128)(2,1)}), bf16[256,1536]{1,0:T(8,128)(2,1)}) %reduce-scatter.7.cloned.1.call-update) | async-done | bytes 786448 | tf_op jit(solution)/shard_map/reduce_scatter | solution.py:280
  912.2 68.2 %reduce-scatter.5.cloned.1.call-done = bf16[256,1536]{1,0:T(8,128)(2,1)} async-done(((bf16[2048,1536]{1,0:T(8,128)(2,1)}), bf16[256,1536]{1,0:T(8,128)(2,1)}) %reduce-scatter.5.cloned.1.call-update) | async-done | bytes 786448 | tf_op jit(solution)/shard_map/reduce_scatter | solution.py:259
  1008.2 2550.7 %while.35 = (s32[]{:T(128)}, f32[8,261,2,96]{3,1,2,0:T(8,128)}, f32[8,1034,2,96]{1,3,2,0:T(8,128)}, f32[8,1024,2,96]{1,3,2,0:T(8,128)}, f32[8,2,6,11]{3,1,0,2:T(...) while((s32[]{:T(128)}, f32[8,261,2,96]{3,1,2,0:T(8,128)}, ...), condition=%wide.region_83.84_spmd.clone, body=%wide.region_13.83_spmd.clone.sunk | while | flops 1772737280 | bytes 370601792 | solution.py:304
  1041.3 36.7 multiply_reduce_fusion.77
  1078.0 11.8 multiply_reduce_fusion.78
  1163.3 124.6 %multiply_multiply_fusion.4 = f32[2,261,1034]{2,1,0:T(8,128)S(1)} fusion(f32[2,256,1024]{2,1,0:T(8,128)} %get-tuple-element.1464, f32[261,1034]{1,0:T(8,128)} %fusion.360, f32[2]{0:T(128)} %get-tuple-element.1396, f32[2]{0:T(128)} %get-tuple-element.1397, f32[2]{0:T(128)} %get-tuple-element.1398, f32[2]{0:T(128)} %get-tuple-element.1399, ...), kind=kLoop, calls=%fused_computation.436.clone.1 | loop fusion | flops 71786448 | bytes 5336168 | tf_op jit(solution)/shard_map/while/body/eval_jaxpr/mul | solution.py:121
  1356.6 36.7 multiply_reduce_fusion.77
  1393.3 11.8 multiply_reduce_fusion.78
  1478.6 124.6 %multiply_multiply_fusion.4 = f32[2,261,1034]{2,1,0:T(8,128)S(1)} fusion(f32[2,256,1024]{2,1,0:T(8,128)} %get-tuple-element.1464, f32[261,1034]{1,0:T(8,128)} %fusion.360, f32[2]{0:T(128)} %get-tuple-element.1396, f32[2]{0:T(128)} %get-tuple-element.1397, f32[2]{0:T(128)} %get-tuple-element.1398, f32[2]{0:T(128)} %get-tuple-element.1399, ...), kind=kLoop, calls=%fused_computation.436.clone.1 | loop fusion | flops 71786448 | bytes 5336168 | tf_op jit(solution)/shard_map/while/body/eval_jaxpr/mul | solution.py:121
  1671.8 36.7 multiply_reduce_fusion.77
  1708.5 11.8 multiply_reduce_fusion.78
  1772.0 11.3 multiply_reduce_fusion.81
  1793.8 124.6 %multiply_multiply_fusion.4 = f32[2,261,1034]{2,1,0:T(8,128)S(1)} fusion(f32[2,256,1024]{2,1,0:T(8,128)} %get-tuple-element.1464, f32[261,1034]{1,0:T(8,128)} %fusion.360, f32[2]{0:T(128)} %get-tuple-element.1396, f32[2]{0:T(128)} %get-tuple-element.1397, f32[2]{0:T(128)} %get-tuple-element.1398, f32[2]{0:T(128)} %get-tuple-element.1399, ...), kind=kLoop, calls=%fused_computation.436.clone.1 | loop fusion | flops 71786448 | bytes 5336168 | tf_op jit(solution)/shard_map/while/body/eval_jaxpr/mul | solution.py:121
  1987.1 36.7 multiply_reduce_fusion.77
  2023.8 11.8 multiply_reduce_fusion.78
  2109.1 124.6 %multiply_multiply_fusion.4 = f32[2,261,1034]{2,1,0:T(8,128)S(1)} fusion(f32[2,256,1024]{2,1,0:T(8,128)} %get-tuple-element.1464, f32[261,1034]{1,0:T(8,128)} %fusion.360, f32[2]{0:T(128)} %get-tuple-element.1396, f32[2]{0:T(128)} %get-tuple-element.1397, f32[2]{0:T(128)} %get-tuple-element.1398, f32[2]{0:T(128)} %get-tuple-element.1399, ...), kind=kLoop, calls=%fused_computation.436.clone.1 | loop fusion | flops 71786448 | bytes 5336168 | tf_op jit(solution)/shard_map/while/body/eval_jaxpr/mul | solution.py:121
  2302.4 36.7 multiply_reduce_fusion.77
  2339.1 11.8 multiply_reduce_fusion.78
  2424.4 124.6 %multiply_multiply_fusion.4 = f32[2,261,1034]{2,1,0:T(8,128)S(1)} fusion(f32[2,256,1024]{2,1,0:T(8,128)} %get-tuple-element.1464, f32[261,1034]{1,0:T(8,128)} %fusion.360, f32[2]{0:T(128)} %get-tuple-element.1396, f32[2]{0:T(128)} %get-tuple-element.1397, f32[2]{0:T(128)} %get-tuple-element.1398, f32[2]{0:T(128)} %get-tuple-element.1399, ...), kind=kLoop, calls=%fused_computation.436.clone.1 | loop fusion | flops 71786448 | bytes 5336168 | tf_op jit(solution)/shard_map/while/body/eval_jaxpr/mul | solution.py:121
  2617.6 36.7 multiply_reduce_fusion.77
  2654.3 11.8 multiply_reduce_fusion.78
  2739.6 124.6 %multiply_multiply_fusion.4 = f32[2,261,1034]{2,1,0:T(8,128)S(1)} fusion(f32[2,256,1024]{2,1,0:T(8,128)} %get-tuple-element.1464, f32[261,1034]{1,0:T(8,128)} %fusion.360, f32[2]{0:T(128)} %get-tuple-element.1396, f32[2]{0:T(128)} %get-tuple-element.1397, f32[2]{0:T(128)} %get-tuple-element.1398, f32[2]{0:T(128)} %get-tuple-element.1399, ...), kind=kLoop, calls=%fused_computation.436.clone.1 | loop fusion | flops 71786448 | bytes 5336168 | tf_op jit(solution)/shard_map/while/body/eval_jaxpr/mul | solution.py:121
  2932.9 36.7 multiply_reduce_fusion.77
  2969.6 11.8 multiply_reduce_fusion.78
  3054.9 124.6 %multiply_multiply_fusion.4 = f32[2,261,1034]{2,1,0:T(8,128)S(1)} fusion(f32[2,256,1024]{2,1,0:T(8,128)} %get-tuple-element.1464, f32[261,1034]{1,0:T(8,128)} %fusion.360, f32[2]{0:T(128)} %get-tuple-element.1396, f32[2]{0:T(128)} %get-tuple-element.1397, f32[2]{0:T(128)} %get-tuple-element.1398, f32[2]{0:T(128)} %get-tuple-element.1399, ...), kind=kLoop, calls=%fused_computation.436.clone.1 | loop fusion | flops 71786448 | bytes 5336168 | tf_op jit(solution)/shard_map/while/body/eval_jaxpr/mul | solution.py:121
  3248.2 36.7 multiply_reduce_fusion.77
  3284.9 11.8 multiply_reduce_fusion.78
  3370.2 124.6 %multiply_multiply_fusion.4 = f32[2,261,1034]{2,1,0:T(8,128)S(1)} fusion(f32[2,256,1024]{2,1,0:T(8,128)} %get-tuple-element.1464, f32[261,1034]{1,0:T(8,128)} %fusion.360, f32[2]{0:T(128)} %get-tuple-element.1396, f32[2]{0:T(128)} %get-tuple-element.1397, f32[2]{0:T(128)} %get-tuple-element.1398, f32[2]{0:T(128)} %get-tuple-element.1399, ...), kind=kLoop, calls=%fused_computation.436.clone.1 | loop fusion | flops 71786448 | bytes 5336168 | tf_op jit(solution)/shard_map/while/body/eval_jaxpr/mul | solution.py:121
  3591.8 28.7 collective-permute-done.7
  3620.5 38.8 collective-permute-done.6
  3693.2 147.7 %reduce-scatter.9.cloned.1.call-done = bf16[192,4608]{1,0:T(8,128)(2,1)} async-done(((bf16[1536,4608]{1,0:T(8,128)(2,1)}), bf16[192,4608]{1,0:T(8,128)(2,1)}) %reduce-scatter.9.cloned.1.call-update) | async-done | bytes 1769488 | tf_op jit(solution)/shard_map/reduce_scatter | solution.py:339
  3842.2 11.5 fusion.270
  3853.7 40.1 all-reduce.2
  3898.0 100.9 %all-reduce.6.cloned.1.call-done = (bf16[192,4608]{1,0:T(8,128)(2,1)}, bf16[192,1536]{1,0:T(8,128)(2,1)}, bf16[1536,512]{1,0:T(8,128)(2,1)}, bf16[1536,512]{1,0:T(8,128)(2,1)}, bf16[512,1536]{1,0:T(8,128)(2,1)}) async-done(((bf16[192,4608]{1,0:T(8,128)(2,1)}, bf16[192,1536]{1,0:T(8,128)(2,1)}, bf16[1536,512]{1,0:T(8,128)(2,1)}, bf16[1536,512]{1,0:T(8,128)(2,1)}, bf16[512,1536]{1,0:T(8,128)(2,1)}), ...) | async-done | bytes 7077904 | tf_op jit(solution)/shard_map/psum | solution.py:351
  (1975 shorter events, 1423.3 us)
Async XLA Ops:
  7.2 812.5 %copy-start = (bf16[512,1536]{1,0:T(8,128)(2,1)S(1)}, bf16[512,1536]{1,0:T(8,128)(2,1)}, u32[]{:S(2)}) copy-start(bf16[512,1536]{1,0:T(8,128)(2,1)} %param.30) | copy-start | bytes 4718596
  7.2 134.9 %copy-start.64 = (f32[1536]{0:T(1024)S(1)}, f32[1536]{0:T(1024)}, u32[]{:S(2)}) copy-start(f32[1536]{0:T(1024)} %param.25) | copy-start | bytes 18436
  7.2 134.8 %all-gather.5.cloned.1.call-start = ((), (), s32[]{:S(2)}) async-start(), calls=%async_computation.4 | async-start | bytes 15925248 | tf_op jit(solution)/shard_map/all_gather | solution.py:209
  8.0 634.8 %all-gather.7.cloned.1.call-start = ((), (), s32[]{:S(2)}) async-start(), calls=%async_computation.5 | async-start | bytes 5308416 | tf_op jit(solution)/shard_map/all_gather | solution.py:210
  9.3 142.0 %copy-start.72 = (f32[256]{0:T(256)}, f32[256]{0:T(256)S(1)}, u32[]{:S(2)}) copy-start(f32[256]{0:T(256)S(1)} %get-tuple-element.869) | copy-start | bytes 3076
  152.7 14.9 copy-start.77
  152.7 15.0 copy-start.70
  154.1 24.5 collective-permute-start.2
  157.4 61.1 %collective-permute-start.1 = (bf16[256,3072]{1,0:T(8,128)(2,1)}, bf16[256,3072]{1,0:T(8,128)(2,1)}, u32[]{:S(2)}, u32[]{:S(2)}) collective-permute-start(bf16[256,3072]{1,0:T(8,128)(2,1)} %slice.2477), channel_id=1, source_target_pairs={{0,2},{1,3},{2,4},{3,5},{4,6},{5,7},{8,10},{9,11},{10,12},{11,13},... | collective-permute-start | bytes 4718600 | tf_op jit(solution)/shard_map/ppermute | solution.py:14
  159.8 105.6 %collective-permute-start = (bf16[256,3072]{1,0:T(8,128)(2,1)}, bf16[256,3072]{1,0:T(8,128)(2,1)}, u32[]{:S(2)}, u32[]{:S(2)}) collective-permute-start(bf16[256,3072]{1,0:T(8,128)(2,1)} %slice.2477), channel_id=1, source_target_pairs={{0,3},{1,4},{2,5},{3,6},{4,7},{8,11},{9,12},{10,13},{11,14},{12,15... | collective-permute-start | bytes 4718600 | tf_op jit(solution)/shard_map/ppermute | solution.py:14
  162.3 591.8 %all-gather.9.cloned.1.call-start = ((), (), s32[]{:S(2)}) async-start(), calls=%async_computation.6 | async-start | bytes 7077888 | tf_op jit(solution)/shard_map/all_gather | solution.py:255
  165.4 3.6 collective-permute-start.3
  649.5 170.1 %all-gather.11.cloned.1.call-start = ((), (), s32[]{:S(2)}) async-start(), calls=%async_computation.8 | async-start | bytes 7077888 | tf_op jit(solution)/shard_map/all_gather | solution.py:266
  651.8 258.2 %reduce-scatter.7.cloned.1.call-start = ((), (), s32[]{:S(2)}) async-start(), calls=%async_computation.9 | async-start | bytes 7077888 | tf_op jit(solution)/shard_map/reduce_scatter | solution.py:280
  841.4 139.0 %reduce-scatter.5.cloned.1.call-start = ((), (), s32[]{:S(2)}) async-start(), calls=%async_computation.7 | async-start | bytes 7077888 | tf_op jit(solution)/shard_map/reduce_scatter | solution.py:259
  848.4 61.6 %copy-start.12 = (f32[256,1536]{1,0:T(8,128)S(1)}, f32[256,1536]{1,0:T(8,128)}, u32[]{:S(2)}) copy-start(f32[256,1536]{1,0:T(8,128)} %copy-done.11) | copy-start | bytes 4718596
  848.4 2844.7 %reduce-scatter.11.cloned.1.call-start = ((), (), s32[]{:S(2)}) async-start(), calls=%async_computation.11 | async-start | bytes 5308416 | tf_op jit(solution)/shard_map/reduce_scatter | solution.py:342
  1008.2 2832.7 %reduce-scatter.9.cloned.1.call-start = ((), (), s32[]{:S(2)}) async-start(), calls=%async_computation.10 | async-start | bytes 15925248 | tf_op jit(solution)/shard_map/reduce_scatter | solution.py:339
  1141.5 11.3 copy-start.2
  1287.9 50.7 %copy-start.68 = (f32[2]{0:T(128)S(1)}, f32[2]{0:T(128)}, u32[]{:S(2)}) copy-start(f32[2]{0:T(128)} %get-tuple-element.1468) | copy-start | bytes 28 | tf_op jit(solution)/shard_map/while
  1287.9 50.7 %copy-start.69 = (f32[2]{0:T(128)S(1)}, f32[2]{0:T(128)}, u32[]{:S(2)}) copy-start(f32[2]{0:T(128)} %get-tuple-element.1466) | copy-start | bytes 28 | tf_op jit(solution)/shard_map/while
  1456.8 11.3 copy-start.2
  1603.2 50.7 %copy-start.68 = (f32[2]{0:T(128)S(1)}, f32[2]{0:T(128)}, u32[]{:S(2)}) copy-start(f32[2]{0:T(128)} %get-tuple-element.1468) | copy-start | bytes 28 | tf_op jit(solution)/shard_map/while
  1603.2 50.7 %copy-start.69 = (f32[2]{0:T(128)S(1)}, f32[2]{0:T(128)}, u32[]{:S(2)}) copy-start(f32[2]{0:T(128)} %get-tuple-element.1466) | copy-start | bytes 28 | tf_op jit(solution)/shard_map/while
  1918.5 50.7 %copy-start.68 = (f32[2]{0:T(128)S(1)}, f32[2]{0:T(128)}, u32[]{:S(2)}) copy-start(f32[2]{0:T(128)} %get-tuple-element.1468) | copy-start | bytes 28 | tf_op jit(solution)/shard_map/while
  1918.5 50.7 %copy-start.69 = (f32[2]{0:T(128)S(1)}, f32[2]{0:T(128)}, u32[]{:S(2)}) copy-start(f32[2]{0:T(128)} %get-tuple-element.1466) | copy-start | bytes 28 | tf_op jit(solution)/shard_map/while
  2233.7 50.7 %copy-start.68 = (f32[2]{0:T(128)S(1)}, f32[2]{0:T(128)}, u32[]{:S(2)}) copy-start(f32[2]{0:T(128)} %get-tuple-element.1468) | copy-start | bytes 28 | tf_op jit(solution)/shard_map/while
  2233.7 50.7 %copy-start.69 = (f32[2]{0:T(128)S(1)}, f32[2]{0:T(128)}, u32[]{:S(2)}) copy-start(f32[2]{0:T(128)} %get-tuple-element.1466) | copy-start | bytes 28 | tf_op jit(solution)/shard_map/while
  2549.0 50.7 %copy-start.68 = (f32[2]{0:T(128)S(1)}, f32[2]{0:T(128)}, u32[]{:S(2)}) copy-start(f32[2]{0:T(128)} %get-tuple-element.1468) | copy-start | bytes 28 | tf_op jit(solution)/shard_map/while
  2549.0 50.7 %copy-start.69 = (f32[2]{0:T(128)S(1)}, f32[2]{0:T(128)}, u32[]{:S(2)}) copy-start(f32[2]{0:T(128)} %get-tuple-element.1466) | copy-start | bytes 28 | tf_op jit(solution)/shard_map/while
  2864.2 50.7 %copy-start.68 = (f32[2]{0:T(128)S(1)}, f32[2]{0:T(128)}, u32[]{:S(2)}) copy-start(f32[2]{0:T(128)} %get-tuple-element.1468) | copy-start | bytes 28 | tf_op jit(solution)/shard_map/while
  2864.2 50.7 %copy-start.69 = (f32[2]{0:T(128)S(1)}, f32[2]{0:T(128)}, u32[]{:S(2)}) copy-start(f32[2]{0:T(128)} %get-tuple-element.1466) | copy-start | bytes 28 | tf_op jit(solution)/shard_map/while
  3179.5 50.7 %copy-start.68 = (f32[2]{0:T(128)S(1)}, f32[2]{0:T(128)}, u32[]{:S(2)}) copy-start(f32[2]{0:T(128)} %get-tuple-element.1468) | copy-start | bytes 28 | tf_op jit(solution)/shard_map/while
  3179.5 50.7 %copy-start.69 = (f32[2]{0:T(128)S(1)}, f32[2]{0:T(128)}, u32[]{:S(2)}) copy-start(f32[2]{0:T(128)} %get-tuple-element.1466) | copy-start | bytes 28 | tf_op jit(solution)/shard_map/while
  3494.8 50.7 %copy-start.68 = (f32[2]{0:T(128)S(1)}, f32[2]{0:T(128)}, u32[]{:S(2)}) copy-start(f32[2]{0:T(128)} %get-tuple-element.1468) | copy-start | bytes 28 | tf_op jit(solution)/shard_map/while
  3494.8 50.7 %copy-start.69 = (f32[2]{0:T(128)S(1)}, f32[2]{0:T(128)}, u32[]{:S(2)}) copy-start(f32[2]{0:T(128)} %get-tuple-element.1466) | copy-start | bytes 28 | tf_op jit(solution)/shard_map/while
  3579.2 12.6 collective-permute-start.5
  3580.5 40.1 collective-permute-start.7
  3581.8 77.6 %collective-permute-start.6 = (bf16[256,3072]{0,1:T(8,128)(2,1)}, bf16[256,3072]{0,1:T(8,128)(2,1)}, u32[]{:S(2)}, u32[]{:S(2)}) collective-permute-start(bf16[256,3072]{0,1:T(8,128)(2,1)} %get-tuple-element.859), channel_id=1, source_target_pairs={{2,0},{3,1},{4,2},{5,3},{6,4},{7,5},{10,8},{11,9},{12,10},{13,11},... | collective-permute-start | bytes 4718600 | tf_op jit(solution)/shard_map/ppermute | solution.py:14
  3587.7 3.8 collective-permute-start.4
  3591.7 71.6 %copy-start.15 = (bf16[1,256,1536]{2,1,0:T(8,128)(2,1)S(1)}, bf16[1,256,1536]{2,1,0:T(8,128)(2,1)}, u32[]{:S(2)}) copy-start(bf16[1,256,1536]{2,1,0:T(8,128)(2,1)} %param.18) | copy-start | bytes 2359300
  3591.8 71.5 %copy-start.20 = (bf16[251,8,2,96]{0,3,2,1:T(8,128)(2,1)S(1)}, bf16[251,8,2,96]{0,3,2,1:T(8,128)(2,1)}, u32[]{:S(2)}) copy-start(bf16[251,8,2,96]{0,3,2,1:T(8,128)(2,1)} %slice.3701) | copy-start | bytes 2313220
  3591.8 71.5 %copy-start.65 = (f32[1536]{0:T(1024)S(1)}, f32[1536]{0:T(1024)}, u32[]{:S(2)}) copy-start(f32[1536]{0:T(1024)} %param.25) | copy-start | bytes 18436
  3591.8 71.5 %copy-start.73 = (f32[256]{0:T(256)S(1)}, f32[256]{0:T(256)}, u32[]{:S(2)}) copy-start(f32[256]{0:T(256)} %copy-done.72) | copy-start | bytes 3076
  3672.5 326.4 %all-reduce.6.cloned.1.call-start = ((), (), s32[]{:S(2)}) async-start(), calls=%async_computation.12 | async-start | bytes 14155776 | tf_op jit(solution)/shard_map/psum | solution.py:351
  3672.6 16.0 slice-start.1
  3842.2 11.5 copy-start.71
  3842.2 53.1 %copy-start.8 = (f32[256,1536]{1,0:T(8,128)S(1)}, f32[256,1536]{1,0:T(8,128)}, u32[]{:S(2)}) copy-start(f32[256,1536]{1,0:T(8,128)} %copy-done.7) | copy-start | bytes 4718596
  (393 other events, 3093.1 us)
Sparse Core Ops, SparseCore 0:
  9.7 132.3 all-gather.4
  162.4 82.5 all-gather.6
  649.7 104.4 all-gather.8
  756.2 63.4 all-gather.10
  841.5 68.4 reduce-scatter.6
  912.1 68.1 reduce-scatter.4
  1008.3 53.3 reduce-scatter.10
  3672.7 168.1 reduce-scatter.8
  3846.3 152.5 all-reduce.5
where the time goes:
time: 4040 us; the launch traced here: 4020 us
  other arithmetic  2010 us (50%)
  local copies, waits for them, and re-layouts  853 us (21%)
  waiting for transfers between devices  821 us (20%)
  matrix products  225 us (6%)
    mul x8, other arithmetic, attend_group_back(): dlogits = convolve_back(dconv, kernel_g) * mask_ext * score_scale  997 us
    another operation x576, local copies, waits for them, and re-layouts, kernel_grads(): entries.append(jnp.stack(line_sums, axis=-1))  678 us
    reduce_sum x32, other arithmetic, kernel_grads(): line_sums.append(jnp.sum(grads * window_part, axis=(1, 2)))  334 us
    reduce_sum x8, other arithmetic, attend_group_back(): dconv = prob * (dprob - jnp.sum(prob * dprob, axis=-1, keepdims=True))  294 us
    reduce_max x8, other arithmetic, attend_group(): peak = jnp.max(jnp.where(allowed, conv, -1e+30), axis=-1, keepdims=True)  277 us
    ppermute x8, waiting for transfers between devices, from_behind(): return lax.ppermute(x, axis, pairs)  155 us
    reduce_scatter x1, waiting for transfers between devices, on_device(): lax.psum_scatter(whole_input_grad.astype(jnp.bfloat16), 'seq', scatter_di...  148 us
    all_gather x1, waiting for transfers between devices, on_device(): lax.all_gather(input_weight, 'seq', axis=0, tiled=True)  133 us
  transfers between devices with their start and end apart: 17, of which 12 were waited for; matrix products, arithmetic and copies ran while one was open for 74% of the time, Pallas kernels for 0%

commit v1 on v0

--- a/solution.py
+++ b/solution.py
@@ -252,7 +252,12 @@
     normed_mid = (resid * second_scale * second_gain).astype(jnp.bfloat16)
     dmlp = (row_valid * grad_out).astype(jnp.bfloat16)
     contract_rows = (((0,), (0,)), ((), ()))
-    inputs_all = lax.all_gather(normed_mid, "seq", axis=0, tiled=True)
+    ring = [normed_mid]
+    for hop in range(7):
+        ring.append(lax.ppermute(ring[-1], "seq", [(dev, (dev + 1) % 8) for dev in range(8)]))
+    inputs_all = jnp.roll(
+        jnp.concatenate(ring[::-1], axis=0), (lax.axis_index("seq") + 1) * ring[0].shape[0], axis=0
+    )
     gate = jnp.dot(inputs_all, gate_weight, preferred_element_type=jnp.float32)
     up_proj = jnp.dot(inputs_all, up_weight, preferred_element_type=jnp.float32)
     hidden = (jax.nn.silu(gate) * up_proj).astype(jnp.bfloat16)

time: 4040 us -> 2980 us (0.74)
  other arithmetic: 2010 us -> 1370 us
  local copies, waits for them, and re-layouts: 853 us -> 441 us
  starting transfers between devices: 16.5 us -> 118 us
  waiting for transfers between devices: 821 us -> 723 us
    mul x8, other arithmetic: 997 us -> 356 us  [attend_group_back(): dlogits = convolve_back(dconv, kernel_g) * mask_ext * score_scale]
    another operation x576, local copies, waits for them, and re-layouts: 678 us -> 235 us  [kernel_grads(): entries.append(jnp.stack(line_sums, axis=-1))]
    all_gather x1 -> x0, waiting for transfers between devices: 102 us -> none  [on_device(): inputs_all = lax.all_gather(normed_mid, 'seq', axis=0, tiled=True)]
    ppermute x0 -> x7, starting transfers between devices: none -> 101 us  [on_device(): lax.ppermute(ring[-1], 'seq', [(dev, (dev + 1) % 8) for dev in range(8)])]
    all_gather x1, waiting for transfers between devices: 51.8 us -> 0.01 us  [on_device(): dmlp_all = lax.all_gather(dmlp, 'seq', axis=0, tiled=True)]
  transfers between devices with their start and end apart: 17 -> 23, of which waited for: 12 -> 17; matrix products, arithmetic and copies ran while one was open for 74% -> 66% of each run, Pallas kernels for 0% -> 0%
where the time goes in v1:
time: 2980 us; the launch traced here: 2970 us
  other arithmetic  1370 us (46%)
  waiting for transfers between devices  723 us (24%)
  local copies, waits for them, and re-layouts  441 us (15%)
  matrix products  246 us (8%)
  starting transfers between devices  118 us (4%)
  blocking collectives  40.1 us (1%)
    mul x8, other arithmetic, attend_group_back(): dlogits = convolve_back(dconv, kernel_g) * mask_ext * score_scale  356 us
    reduce_sum x32, other arithmetic, kernel_grads(): line_sums.append(jnp.sum(grads * window_part, axis=(1, 2)))  335 us
    reduce_sum x8, other arithmetic, attend_group_back(): dconv = prob * (dprob - jnp.sum(prob * dprob, axis=-1, keepdims=True))  294 us
    reduce_max x8, other arithmetic, attend_group(): peak = jnp.max(jnp.where(allowed, conv, -1e+30), axis=-1, keepdims=True)  277 us
    another operation x576, local copies, waits for them, and re-layouts, kernel_grads(): entries.append(jnp.stack(line_sums, axis=-1))  235 us
    ppermute x8, waiting for transfers between devices, from_behind(): return lax.ppermute(x, axis, pairs)  160 us
    reduce_scatter x1, waiting for transfers between devices, on_device(): lax.psum_scatter(whole_input_grad.astype(jnp.bfloat16), 'seq', scatter_di...  157 us
    all_gather x1, waiting for transfers between devices, on_device(): lax.all_gather(input_weight, 'seq', axis=0, tiled=True)  132 us
  transfers between devices with their start and end apart: 23, of which 17 were waited for; matrix products, arithmetic and copies ran while one was open for 66% of the time, Pallas kernels for 0%

profile of v1, /device:TPU:0, one launch (start us, length us, event | category | flops | bytes accessed | tf_op | source)
XLA Modules:
  0.0 2971.2 jit_solution(3652721059938424560)
XLA Ops:
  9.7 132.3 %all-gather.4.cloned.1.call-done = bf16[1536,4608]{1,0:T(8,128)(2,1)} async-done(((bf16[192,4608]{1,0:T(8,128)(2,1)}), bf16[1536,4608]{1,0:T(8,128)(2,1)}) %all-gather.4.cloned.1.call-update) | async-done | bytes 14155792 | tf_op jit(solution)/shard_map/all_gather | solution.py:209
  175.5 46.3 %collective-permute-done = bf16[256,3072]{1,0:T(8,128)(2,1)} collective-permute-done((bf16[256,3072]{1,0:T(8,128)(2,1)}, bf16[256,3072]{1,0:T(8,128)(2,1)}, u32[]{:S(2)}, u32[]{:S(2)}) %collective-permute-start) | collective-permute-done | bytes 1572896 | tf_op jit(solution)/shard_map/ppermute | solution.py:14
  221.8 54.2 %collective-permute-done.1 = bf16[256,3072]{1,0:T(8,128)(2,1)} collective-permute-done((bf16[256,3072]{1,0:T(8,128)(2,1)}, bf16[256,3072]{1,0:T(8,128)(2,1)}, u32[]{:S(2)}, u32[]{:S(2)}) %collective-permute-start.1) | collective-permute-done | bytes 1572896 | tf_op jit(solution)/shard_map/ppermute | solution.py:14
  297.7 337.2 %while.34 = (s32[]{:T(128)}, f32[8,256,2,96]{1,3,2,0:T(8,128)}, f32[8,2,256,1]{2,1,3,0:T(2,128)}, bf16[8,1024,2,96]{1,3,2,0:T(8,128)(2,1)}, f32[8,2,2]{2,1,0:T(2...) while((s32[]{:T(128)}, f32[8,256,2,96]{1,3,2,0:T(8,128)}, ...), condition=%wide.region_4.5_spmd.clone, body=%wide.region_1.4_spmd.clone.sunk | while | flops 281692032 | bytes 160720112 | solution.py:238
  300.7 34.6 %select_reduce_fusion.2 = (f32[2,256]{1,0:T(2,128)S(1)}, f32[2,256,1024]{2,1,0:T(8,128)S(1)}) fusion(pred[256,1024]{1,0:T(8,128)(4,1)S(1)} %broadcast_compare_fusion.5, f32[2,261,1034]{2,1,0:T(8,128)S(1)} %convolution_multiply_fusion.5, f32[2]{0:T(128)S(1)} %get-tuple-element.1300, f32[2]{0:T(128)S(1)} %get-tuple-element.1301, ...), kind=kLoop, calls=%fused_computation.136.clone.1 | loop fusion | flops 69729792 | bytes 140773904 | tf_op jit(solution)/shard_map/while/body/eval_jaxpr/reduce_max | solution.py:79
  342.8 34.6 %select_reduce_fusion.2 = (f32[2,256]{1,0:T(2,128)S(1)}, f32[2,256,1024]{2,1,0:T(8,128)S(1)}) fusion(pred[256,1024]{1,0:T(8,128)(4,1)S(1)} %broadcast_compare_fusion.5, f32[2,261,1034]{2,1,0:T(8,128)S(1)} %convolution_multiply_fusion.5, f32[2]{0:T(128)S(1)} %get-tuple-element.1300, f32[2]{0:T(128)S(1)} %get-tuple-element.1301, ...), kind=kLoop, calls=%fused_computation.136.clone.1 | loop fusion | flops 69729792 | bytes 140773904 | tf_op jit(solution)/shard_map/while/body/eval_jaxpr/reduce_max | solution.py:79
  384.9 34.6 %select_reduce_fusion.2 = (f32[2,256]{1,0:T(2,128)S(1)}, f32[2,256,1024]{2,1,0:T(8,128)S(1)}) fusion(pred[256,1024]{1,0:T(8,128)(4,1)S(1)} %broadcast_compare_fusion.5, f32[2,261,1034]{2,1,0:T(8,128)S(1)} %convolution_multiply_fusion.5, f32[2]{0:T(128)S(1)} %get-tuple-element.1300, f32[2]{0:T(128)S(1)} %get-tuple-element.1301, ...), kind=kLoop, calls=%fused_computation.136.clone.1 | loop fusion | flops 69729792 | bytes 140773904 | tf_op jit(solution)/shard_map/while/body/eval_jaxpr/reduce_max | solution.py:79
  427.1 34.6 %select_reduce_fusion.2 = (f32[2,256]{1,0:T(2,128)S(1)}, f32[2,256,1024]{2,1,0:T(8,128)S(1)}) fusion(pred[256,1024]{1,0:T(8,128)(4,1)S(1)} %broadcast_compare_fusion.5, f32[2,261,1034]{2,1,0:T(8,128)S(1)} %convolution_multiply_fusion.5, f32[2]{0:T(128)S(1)} %get-tuple-element.1300, f32[2]{0:T(128)S(1)} %get-tuple-element.1301, ...), kind=kLoop, calls=%fused_computation.136.clone.1 | loop fusion | flops 69729792 | bytes 140773904 | tf_op jit(solution)/shard_map/while/body/eval_jaxpr/reduce_max | solution.py:79
  469.2 34.6 %select_reduce_fusion.2 = (f32[2,256]{1,0:T(2,128)S(1)}, f32[2,256,1024]{2,1,0:T(8,128)S(1)}) fusion(pred[256,1024]{1,0:T(8,128)(4,1)S(1)} %broadcast_compare_fusion.5, f32[2,261,1034]{2,1,0:T(8,128)S(1)} %convolution_multiply_fusion.5, f32[2]{0:T(128)S(1)} %get-tuple-element.1300, f32[2]{0:T(128)S(1)} %get-tuple-element.1301, ...), kind=kLoop, calls=%fused_computation.136.clone.1 | loop fusion | flops 69729792 | bytes 140773904 | tf_op jit(solution)/shard_map/while/body/eval_jaxpr/reduce_max | solution.py:79
  511.3 34.6 %select_reduce_fusion.2 = (f32[2,256]{1,0:T(2,128)S(1)}, f32[2,256,1024]{2,1,0:T(8,128)S(1)}) fusion(pred[256,1024]{1,0:T(8,128)(4,1)S(1)} %broadcast_compare_fusion.5, f32[2,261,1034]{2,1,0:T(8,128)S(1)} %convolution_multiply_fusion.5, f32[2]{0:T(128)S(1)} %get-tuple-element.1300, f32[2]{0:T(128)S(1)} %get-tuple-element.1301, ...), kind=kLoop, calls=%fused_computation.136.clone.1 | loop fusion | flops 69729792 | bytes 140773904 | tf_op jit(solution)/shard_map/while/body/eval_jaxpr/reduce_max | solution.py:79
  553.5 34.6 %select_reduce_fusion.2 = (f32[2,256]{1,0:T(2,128)S(1)}, f32[2,256,1024]{2,1,0:T(8,128)S(1)}) fusion(pred[256,1024]{1,0:T(8,128)(4,1)S(1)} %broadcast_compare_fusion.5, f32[2,261,1034]{2,1,0:T(8,128)S(1)} %convolution_multiply_fusion.5, f32[2]{0:T(128)S(1)} %get-tuple-element.1300, f32[2]{0:T(128)S(1)} %get-tuple-element.1301, ...), kind=kLoop, calls=%fused_computation.136.clone.1 | loop fusion | flops 69729792 | bytes 140773904 | tf_op jit(solution)/shard_map/while/body/eval_jaxpr/reduce_max | solution.py:79
  595.6 34.6 %select_reduce_fusion.2 = (f32[2,256]{1,0:T(2,128)S(1)}, f32[2,256,1024]{2,1,0:T(8,128)S(1)}) fusion(pred[256,1024]{1,0:T(8,128)(4,1)S(1)} %broadcast_compare_fusion.5, f32[2,261,1034]{2,1,0:T(8,128)S(1)} %convolution_multiply_fusion.5, f32[2]{0:T(128)S(1)} %get-tuple-element.1300, f32[2]{0:T(128)S(1)} %get-tuple-element.1301, ...), kind=kLoop, calls=%fused_computation.136.clone.1 | loop fusion | flops 69729792 | bytes 140773904 | tf_op jit(solution)/shard_map/while/body/eval_jaxpr/reduce_max | solution.py:79
  659.5 52.1 %collective-permute-start.4 = (bf16[256,1536]{1,0:T(8,128)(2,1)S(1)}, bf16[256,1536]{1,0:T(8,128)(2,1)S(1)}, u32[]{:S(2)}, u32[]{:S(2)}) collective-permute-start(bf16[256,1536]{1,0:T(8,128)(2,1)S(1)} %multiply_convert_fusion.5), channel_id=1, source_target_pairs={{0,1},{1,2},{2,3},{3,4},{4,5},{5,6},{6,7},{7,0},{8,9},{9,10},{10,1... | collective-permute-start | bytes 2359304 | tf_op jit(solution)/shard_map/ppermute | solution.py:257
  728.5 13.4 collective-permute-start.6
  848.7 74.6 %reduce-scatter.7.cloned.1.call-done = bf16[256,1536]{1,0:T(8,128)(2,1)} async-done(((bf16[2048,1536]{1,0:T(8,128)(2,1)}), bf16[256,1536]{1,0:T(8,128)(2,1)}) %reduce-scatter.7.cloned.1.call-update) | async-done | bytes 786448 | tf_op jit(solution)/shard_map/reduce_scatter | solution.py:285
  925.4 68.2 %reduce-scatter.5.cloned.1.call-done = bf16[256,1536]{1,0:T(8,128)(2,1)} async-done(((bf16[2048,1536]{1,0:T(8,128)(2,1)}), bf16[256,1536]{1,0:T(8,128)(2,1)}) %reduce-scatter.5.cloned.1.call-update) | async-done | bytes 786448 | tf_op jit(solution)/shard_map/reduce_scatter | solution.py:264
  1023.1 1489.3 %while.35 = (s32[]{:T(128)}, f32[8,261,2,96]{3,1,2,0:T(8,128)}, f32[8,1034,2,96]{1,3,2,0:T(8,128)}, f32[8,1024,2,96]{1,3,2,0:T(8,128)}, f32[8,2,6,11]{3,1,0,2:T(...) while((s32[]{:T(128)}, f32[8,261,2,96]{3,1,2,0:T(8,128)}, ...), condition=%wide.region_83.84_spmd.clone, body=%wide.region_13.83_spmd.clone.sunk | while | flops 1772737280 | bytes 377415552 | solution.py:309
  1034.2 36.7 %multiply_reduce_fusion.77 = (f32[2,256]{1,0:T(2,128)S(1)}, f32[2,256,1024]{2,1,0:T(8,128)S(1)}) fusion(f32[256,1024]{1,0:T(8,128)} %get-tuple-element.1392, f32[2]{0:T(128)} %get-tuple-element.1393, f32[256,1024]{1,0:T(8,128)S(1)} %get-tuple-element.1394, f32[2]{0:T(128)} %get-tuple-element.1395, f32[2,256]{1,0:T(2,128)S(1)} %fusion.372, ...), kind=kLoop, calls=%fused_computation.507.clone.1 | loop fusion | flops 72351232 | bytes 142873120 | tf_op jit(solution)/shard_map/while/body/eval_jaxpr/reduce_sum | solution.py:119
  1076.7 12.2 multiply_reduce_fusion.78
  1156.8 44.5 %multiply_multiply_fusion.4 = f32[2,261,1034]{2,1,0:T(8,128)} fusion(f32[2,256,1024]{2,1,0:T(8,128)S(1)} %copy-done.2, f32[261,1034]{1,0:T(8,128)} %fusion.373, f32[2]{0:T(128)S(1)} %get-tuple-element.1396, f32[2]{0:T(128)S(1)} %get-tuple-element.1397, f32[2]{0:T(128)S(1)} %get-tuple-element.1398, f32[2]{0:T(128)S(1)} %get-tuple-element.1399, ...), kind=kLoop, calls=%fused_computation.436.clone.1 | loop fusion | flops 71786448 | bytes 5336168 | tf_op jit(solution)/shard_map/while/body/eval_jaxpr/mul | solution.py:121
  1219.4 36.7 %multiply_reduce_fusion.77 = (f32[2,256]{1,0:T(2,128)S(1)}, f32[2,256,1024]{2,1,0:T(8,128)S(1)}) fusion(f32[256,1024]{1,0:T(8,128)} %get-tuple-element.1392, f32[2]{0:T(128)} %get-tuple-element.1393, f32[256,1024]{1,0:T(8,128)S(1)} %get-tuple-element.1394, f32[2]{0:T(128)} %get-tuple-element.1395, f32[2,256]{1,0:T(2,128)S(1)} %fusion.372, ...), kind=kLoop, calls=%fused_computation.507.clone.1 | loop fusion | flops 72351232 | bytes 142873120 | tf_op jit(solution)/shard_map/while/body/eval_jaxpr/reduce_sum | solution.py:119
  1261.8 12.2 multiply_reduce_fusion.78
  1296.2 10.9 multiply_reduce_fusion.80
  1342.0 44.5 %multiply_multiply_fusion.4 = f32[2,261,1034]{2,1,0:T(8,128)} fusion(f32[2,256,1024]{2,1,0:T(8,128)S(1)} %copy-done.2, f32[261,1034]{1,0:T(8,128)} %fusion.373, f32[2]{0:T(128)S(1)} %get-tuple-element.1396, f32[2]{0:T(128)S(1)} %get-tuple-element.1397, f32[2]{0:T(128)S(1)} %get-tuple-element.1398, f32[2]{0:T(128)S(1)} %get-tuple-element.1399, ...), kind=kLoop, calls=%fused_computation.436.clone.1 | loop fusion | flops 71786448 | bytes 5336168 | tf_op jit(solution)/shard_map/while/body/eval_jaxpr/mul | solution.py:121
  1404.6 36.7 %multiply_reduce_fusion.77 = (f32[2,256]{1,0:T(2,128)S(1)}, f32[2,256,1024]{2,1,0:T(8,128)S(1)}) fusion(f32[256,1024]{1,0:T(8,128)} %get-tuple-element.1392, f32[2]{0:T(128)} %get-tuple-element.1393, f32[256,1024]{1,0:T(8,128)S(1)} %get-tuple-element.1394, f32[2]{0:T(128)} %get-tuple-element.1395, f32[2,256]{1,0:T(2,128)S(1)} %fusion.372, ...), kind=kLoop, calls=%fused_computation.507.clone.1 | loop fusion | flops 72351232 | bytes 142873120 | tf_op jit(solution)/shard_map/while/body/eval_jaxpr/reduce_sum | solution.py:119
  1447.0 12.2 multiply_reduce_fusion.78
  1527.1 44.5 %multiply_multiply_fusion.4 = f32[2,261,1034]{2,1,0:T(8,128)} fusion(f32[2,256,1024]{2,1,0:T(8,128)S(1)} %copy-done.2, f32[261,1034]{1,0:T(8,128)} %fusion.373, f32[2]{0:T(128)S(1)} %get-tuple-element.1396, f32[2]{0:T(128)S(1)} %get-tuple-element.1397, f32[2]{0:T(128)S(1)} %get-tuple-element.1398, f32[2]{0:T(128)S(1)} %get-tuple-element.1399, ...), kind=kLoop, calls=%fused_computation.436.clone.1 | loop fusion | flops 71786448 | bytes 5336168 | tf_op jit(solution)/shard_map/while/body/eval_jaxpr/mul | solution.py:121
  1589.8 36.7 %multiply_reduce_fusion.77 = (f32[2,256]{1,0:T(2,128)S(1)}, f32[2,256,1024]{2,1,0:T(8,128)S(1)}) fusion(f32[256,1024]{1,0:T(8,128)} %get-tuple-element.1392, f32[2]{0:T(128)} %get-tuple-element.1393, f32[256,1024]{1,0:T(8,128)S(1)} %get-tuple-element.1394, f32[2]{0:T(128)} %get-tuple-element.1395, f32[2,256]{1,0:T(2,128)S(1)} %fusion.372, ...), kind=kLoop, calls=%fused_computation.507.clone.1 | loop fusion | flops 72351232 | bytes 142873120 | tf_op jit(solution)/shard_map/while/body/eval_jaxpr/reduce_sum | solution.py:119
  1632.2 12.2 multiply_reduce_fusion.78
  1712.3 44.5 %multiply_multiply_fusion.4 = f32[2,261,1034]{2,1,0:T(8,128)} fusion(f32[2,256,1024]{2,1,0:T(8,128)S(1)} %copy-done.2, f32[261,1034]{1,0:T(8,128)} %fusion.373, f32[2]{0:T(128)S(1)} %get-tuple-element.1396, f32[2]{0:T(128)S(1)} %get-tuple-element.1397, f32[2]{0:T(128)S(1)} %get-tuple-element.1398, f32[2]{0:T(128)S(1)} %get-tuple-element.1399, ...), kind=kLoop, calls=%fused_computation.436.clone.1 | loop fusion | flops 71786448 | bytes 5336168 | tf_op jit(solution)/shard_map/while/body/eval_jaxpr/mul | solution.py:121
  1775.0 36.7 %multiply_reduce_fusion.77 = (f32[2,256]{1,0:T(2,128)S(1)}, f32[2,256,1024]{2,1,0:T(8,128)S(1)}) fusion(f32[256,1024]{1,0:T(8,128)} %get-tuple-element.1392, f32[2]{0:T(128)} %get-tuple-element.1393, f32[256,1024]{1,0:T(8,128)S(1)} %get-tuple-element.1394, f32[2]{0:T(128)} %get-tuple-element.1395, f32[2,256]{1,0:T(2,128)S(1)} %fusion.372, ...), kind=kLoop, calls=%fused_computation.507.clone.1 | loop fusion | flops 72351232 | bytes 142873120 | tf_op jit(solution)/shard_map/while/body/eval_jaxpr/reduce_sum | solution.py:119
  1817.4 12.2 multiply_reduce_fusion.78
  1851.8 10.9 multiply_reduce_fusion.80
  1897.5 44.5 %multiply_multiply_fusion.4 = f32[2,261,1034]{2,1,0:T(8,128)} fusion(f32[2,256,1024]{2,1,0:T(8,128)S(1)} %copy-done.2, f32[261,1034]{1,0:T(8,128)} %fusion.373, f32[2]{0:T(128)S(1)} %get-tuple-element.1396, f32[2]{0:T(128)S(1)} %get-tuple-element.1397, f32[2]{0:T(128)S(1)} %get-tuple-element.1398, f32[2]{0:T(128)S(1)} %get-tuple-element.1399, ...), kind=kLoop, calls=%fused_computation.436.clone.1 | loop fusion | flops 71786448 | bytes 5336168 | tf_op jit(solution)/shard_map/while/body/eval_jaxpr/mul | solution.py:121
  1960.1 36.7 %multiply_reduce_fusion.77 = (f32[2,256]{1,0:T(2,128)S(1)}, f32[2,256,1024]{2,1,0:T(8,128)S(1)}) fusion(f32[256,1024]{1,0:T(8,128)} %get-tuple-element.1392, f32[2]{0:T(128)} %get-tuple-element.1393, f32[256,1024]{1,0:T(8,128)S(1)} %get-tuple-element.1394, f32[2]{0:T(128)} %get-tuple-element.1395, f32[2,256]{1,0:T(2,128)S(1)} %fusion.372, ...), kind=kLoop, calls=%fused_computation.507.clone.1 | loop fusion | flops 72351232 | bytes 142873120 | tf_op jit(solution)/shard_map/while/body/eval_jaxpr/reduce_sum | solution.py:119
  2002.6 12.2 multiply_reduce_fusion.78
  2082.7 44.5 %multiply_multiply_fusion.4 = f32[2,261,1034]{2,1,0:T(8,128)} fusion(f32[2,256,1024]{2,1,0:T(8,128)S(1)} %copy-done.2, f32[261,1034]{1,0:T(8,128)} %fusion.373, f32[2]{0:T(128)S(1)} %get-tuple-element.1396, f32[2]{0:T(128)S(1)} %get-tuple-element.1397, f32[2]{0:T(128)S(1)} %get-tuple-element.1398, f32[2]{0:T(128)S(1)} %get-tuple-element.1399, ...), kind=kLoop, calls=%fused_computation.436.clone.1 | loop fusion | flops 71786448 | bytes 5336168 | tf_op jit(solution)/shard_map/while/body/eval_jaxpr/mul | solution.py:121
  2145.3 36.7 %multiply_reduce_fusion.77 = (f32[2,256]{1,0:T(2,128)S(1)}, f32[2,256,1024]{2,1,0:T(8,128)S(1)}) fusion(f32[256,1024]{1,0:T(8,128)} %get-tuple-element.1392, f32[2]{0:T(128)} %get-tuple-element.1393, f32[256,1024]{1,0:T(8,128)S(1)} %get-tuple-element.1394, f32[2]{0:T(128)} %get-tuple-element.1395, f32[2,256]{1,0:T(2,128)S(1)} %fusion.372, ...), kind=kLoop, calls=%fused_computation.507.clone.1 | loop fusion | flops 72351232 | bytes 142873120 | tf_op jit(solution)/shard_map/while/body/eval_jaxpr/reduce_sum | solution.py:119
  2187.8 12.2 multiply_reduce_fusion.78
  2267.9 44.5 %multiply_multiply_fusion.4 = f32[2,261,1034]{2,1,0:T(8,128)} fusion(f32[2,256,1024]{2,1,0:T(8,128)S(1)} %copy-done.2, f32[261,1034]{1,0:T(8,128)} %fusion.373, f32[2]{0:T(128)S(1)} %get-tuple-element.1396, f32[2]{0:T(128)S(1)} %get-tuple-element.1397, f32[2]{0:T(128)S(1)} %get-tuple-element.1398, f32[2]{0:T(128)S(1)} %get-tuple-element.1399, ...), kind=kLoop, calls=%fused_computation.436.clone.1 | loop fusion | flops 71786448 | bytes 5336168 | tf_op jit(solution)/shard_map/while/body/eval_jaxpr/mul | solution.py:121
  2330.5 36.7 %multiply_reduce_fusion.77 = (f32[2,256]{1,0:T(2,128)S(1)}, f32[2,256,1024]{2,1,0:T(8,128)S(1)}) fusion(f32[256,1024]{1,0:T(8,128)} %get-tuple-element.1392, f32[2]{0:T(128)} %get-tuple-element.1393, f32[256,1024]{1,0:T(8,128)S(1)} %get-tuple-element.1394, f32[2]{0:T(128)} %get-tuple-element.1395, f32[2,256]{1,0:T(2,128)S(1)} %fusion.372, ...), kind=kLoop, calls=%fused_computation.507.clone.1 | loop fusion | flops 72351232 | bytes 142873120 | tf_op jit(solution)/shard_map/while/body/eval_jaxpr/reduce_sum | solution.py:119
  2373.0 12.2 multiply_reduce_fusion.78
  2453.1 44.5 %multiply_multiply_fusion.4 = f32[2,261,1034]{2,1,0:T(8,128)} fusion(f32[2,256,1024]{2,1,0:T(8,128)S(1)} %copy-done.2, f32[261,1034]{1,0:T(8,128)} %fusion.373, f32[2]{0:T(128)S(1)} %get-tuple-element.1396, f32[2]{0:T(128)S(1)} %get-tuple-element.1397, f32[2]{0:T(128)S(1)} %get-tuple-element.1398, f32[2]{0:T(128)S(1)} %get-tuple-element.1399, ...), kind=kLoop, calls=%fused_computation.436.clone.1 | loop fusion | flops 71786448 | bytes 5336168 | tf_op jit(solution)/shard_map/while/body/eval_jaxpr/mul | solution.py:121
  2545.8 52.9 %collective-permute-done.13 = bf16[256,3072]{0,1:T(8,128)(2,1)} collective-permute-done((bf16[256,3072]{0,1:T(8,128)(2,1)}, bf16[256,3072]{0,1:T(8,128)(2,1)}, u32[]{:S(2)}, u32[]{:S(2)}) %collective-permute-start.13) | collective-permute-done | bytes 1572896 | tf_op jit(solution)/shard_map/ppermute | solution.py:14
  2637.7 157.0 %reduce-scatter.9.cloned.1.call-done = bf16[192,4608]{1,0:T(8,128)(2,1)} async-done(((bf16[1536,4608]{1,0:T(8,128)(2,1)}), bf16[192,4608]{1,0:T(8,128)(2,1)}) %reduce-scatter.9.cloned.1.call-update) | async-done | bytes 1769488 | tf_op jit(solution)/shard_map/reduce_scatter | solution.py:344
  2795.6 11.0 fusion.284
  2806.6 40.1 %all-reduce.2 = (f32[16,6,11]{2,0,1:T(8,128)S(1)}, f32[8,2,2]{0,2,1:T(2,128)}, f32[1536]{0:T(1024)}, f32[1536]{0:T(1024)}, f32[1536]{0:T(1024)}) all-reduce(f32[16,6,11]{2,0,1:T(8,128)S(1)} %bitcast.778, f32[8,2,2]{0,2,1:T(2,128)S(1)} %copy.255, f32[1536]{0:T(1024)S(1)} %get-tuple-element.619, ...), channel_id=1, replica_groups=mesh['rep'=4,'seq'=8] {'rep','seq'}, use_global_device_ids=true, to_apply=%region_89.90 | all-reduce | flops 5696 | bytes 45568 | tf_op jit(solution)/shard_map/psum | solution.py:352
  2850.3 102.6 %all-reduce.6.cloned.1.call-done = (bf16[192,4608]{1,0:T(8,128)(2,1)}, bf16[192,1536]{1,0:T(8,128)(2,1)}, bf16[1536,512]{1,0:T(8,128)(2,1)}, bf16[1536,512]{1,0:T(8,128)(2,1)}, bf16[512,1536]{1,0:T(8,128)(2,1)}) async-done(((bf16[192,4608]{1,0:T(8,128)(2,1)}, bf16[192,1536]{1,0:T(8,128)(2,1)}, bf16[1536,512]{1,0:T(8,128)(2,1)}, bf16[1536,512]{1,0:T(8,128)(2,1)}, bf16[512,1536]{1,0:T(8,128)(2,1)}), ...) | async-done | bytes 7077904 | tf_op jit(solution)/shard_map/psum | solution.py:356
  (2733 shorter events, 1085.2 us)
Async XLA Ops:
  7.2 808.8 %copy-start = (bf16[1536,512]{1,0:T(8,128)(2,1)S(1)}, bf16[1536,512]{1,0:T(8,128)(2,1)}, u32[]{:S(2)}) copy-start(bf16[1536,512]{1,0:T(8,128)(2,1)} %param.28) | copy-start | bytes 4718596
  7.2 134.9 %copy-start.115 = (f32[1536]{0:T(1024)S(1)}, f32[1536]{0:T(1024)}, u32[]{:S(2)}) copy-start(f32[1536]{0:T(1024)} %param.25) | copy-start | bytes 18436
  7.2 134.8 %all-gather.4.cloned.1.call-start = ((), (), s32[]{:S(2)}) async-start(), calls=%async_computation.4 | async-start | bytes 15925248 | tf_op jit(solution)/shard_map/all_gather | solution.py:209
  8.0 645.8 %all-gather.6.cloned.1.call-start = ((), (), s32[]{:S(2)}) async-start(), calls=%async_computation.5 | async-start | bytes 5308416 | tf_op jit(solution)/shard_map/all_gather | solution.py:210
  8.7 781.0 %all-gather.8.cloned.1.call-start = ((), (), s32[]{:S(2)}) async-start(), calls=%async_computation.7 | async-start | bytes 7077888 | tf_op jit(solution)/shard_map/all_gather | solution.py:271
  9.7 141.6 %copy-start.123 = (f32[256]{0:T(256)}, f32[256]{0:T(256)S(1)}, u32[]{:S(2)}) copy-start(f32[256]{0:T(256)S(1)} %get-tuple-element.869) | copy-start | bytes 3076
  152.7 12.5 copy-start.134
  154.1 14.3 copy-start.120
  154.1 15.6 copy-start.136
  154.1 67.7 %collective-permute-start = (bf16[256,3072]{1,0:T(8,128)(2,1)}, bf16[256,3072]{1,0:T(8,128)(2,1)}, u32[]{:S(2)}, u32[]{:S(2)}) collective-permute-start(bf16[256,3072]{1,0:T(8,128)(2,1)} %slice.2477), channel_id=1, source_target_pairs={{0,3},{1,4},{2,5},{3,6},{4,7},{8,11},{9,12},{10,13},{11,14},{12,15... | collective-permute-start | bytes 4718600 | tf_op jit(solution)/shard_map/ppermute | solution.py:14
  156.7 119.3 %collective-permute-start.1 = (bf16[256,3072]{1,0:T(8,128)(2,1)}, bf16[256,3072]{1,0:T(8,128)(2,1)}, u32[]{:S(2)}, u32[]{:S(2)}) collective-permute-start(bf16[256,3072]{1,0:T(8,128)(2,1)} %slice.2477), channel_id=1, source_target_pairs={{0,2},{1,3},{2,4},{3,5},{4,6},{5,7},{8,10},{9,11},{10,12},{11,13},... | collective-permute-start | bytes 4718600 | tf_op jit(solution)/shard_map/ppermute | solution.py:14
  161.4 114.6 %collective-permute-start.2 = (bf16[256,3072]{1,0:T(8,128)(2,1)}, bf16[256,3072]{1,0:T(8,128)(2,1)}, u32[]{:S(2)}, u32[]{:S(2)}) collective-permute-start(bf16[256,3072]{1,0:T(8,128)(2,1)} %slice.2477), channel_id=1, source_target_pairs={{0,1},{1,2},{2,3},{3,4},{4,5},{5,6},{6,7},{8,9},{9,10},{10,11},{11... | collective-permute-start | bytes 4718600 | tf_op jit(solution)/shard_map/ppermute | solution.py:14
  165.1 758.2 %reduce-scatter.7.cloned.1.call-start = ((), (), s32[]{:S(2)}) async-start(), calls=%async_computation.8 | async-start | bytes 7077888 | tf_op jit(solution)/shard_map/reduce_scatter | solution.py:285
  166.7 4.2 collective-permute-start.3
  659.5 54.0 %collective-permute-start.4 = (bf16[256,1536]{1,0:T(8,128)(2,1)S(1)}, bf16[256,1536]{1,0:T(8,128)(2,1)S(1)}, u32[]{:S(2)}, u32[]{:S(2)}) collective-permute-start(bf16[256,1536]{1,0:T(8,128)(2,1)S(1)} %multiply_convert_fusion.5), channel_id=1, source_target_pairs={{0,1},{1,2},{2,3},{3,4},{4,5},{5,6},{6,7},{7,0},{8,9},{9,10},{10,1... | collective-permute-start | bytes 2359304 | tf_op jit(solution)/shard_map/ppermute | solution.py:257
  713.5 14.1 collective-permute-start.5
  728.5 15.3 collective-permute-start.6
  744.6 13.5 collective-permute-start.7
  759.0 13.3 collective-permute-start.8
  772.4 13.5 collective-permute-start.9
  785.9 13.5 collective-permute-start.10
  839.8 153.8 %reduce-scatter.5.cloned.1.call-start = ((), (), s32[]{:S(2)}) async-start(), calls=%async_computation.6 | async-start | bytes 7077888 | tf_op jit(solution)/shard_map/reduce_scatter | solution.py:264
  848.0 75.2 %copy-start.12 = (f32[256,1536]{1,0:T(8,128)S(1)}, f32[256,1536]{1,0:T(8,128)}, u32[]{:S(2)}) copy-start(f32[256,1536]{1,0:T(8,128)} %copy-done.10) | copy-start | bytes 4718596
  848.1 145.5 %copy-start.29 = (bf16[1,256,1536]{2,1,0:T(8,128)(2,1)S(1)}, bf16[1,256,1536]{2,1,0:T(8,128)(2,1)}, u32[]{:S(2)}) copy-start(bf16[1,256,1536]{2,1,0:T(8,128)(2,1)} %param.31) | copy-start | bytes 2359300
  848.1 1789.7 %reduce-scatter.11.cloned.1.call-start = ((), (), s32[]{:S(2)}) async-start(), calls=%async_computation.10 | async-start | bytes 5308416 | tf_op jit(solution)/shard_map/reduce_scatter | solution.py:347
  1023.1 1771.7 %reduce-scatter.9.cloned.1.call-start = ((), (), s32[]{:S(2)}) async-start(), calls=%async_computation.9 | async-start | bytes 15925248 | tf_op jit(solution)/shard_map/reduce_scatter | solution.py:344
  1097.1 11.5 copy-start.125
  1130.1 21.4 copy-start.6
  1315.3 21.4 copy-start.6
  1467.5 11.5 copy-start.125
  1500.5 21.4 copy-start.6
  1685.7 21.4 copy-start.6
  1870.9 21.4 copy-start.6
  2056.0 21.4 copy-start.6
  2241.2 21.4 copy-start.6
  2426.4 21.4 copy-start.6
  2532.5 13.3 collective-permute-start.12
  2533.8 64.9 %collective-permute-start.13 = (bf16[256,3072]{0,1:T(8,128)(2,1)}, bf16[256,3072]{0,1:T(8,128)(2,1)}, u32[]{:S(2)}, u32[]{:S(2)}) collective-permute-start(bf16[256,3072]{0,1:T(8,128)(2,1)} %get-tuple-element.859), channel_id=1, source_target_pairs={{2,0},{3,1},{4,2},{5,3},{6,4},{7,5},{10,8},{11,9},{12,10},{13,11},... | collective-permute-start | bytes 4718600 | tf_op jit(solution)/shard_map/ppermute | solution.py:14
  2535.1 68.8 %collective-permute-start.14 = (bf16[256,3072]{0,1:T(8,128)(2,1)}, bf16[256,3072]{0,1:T(8,128)(2,1)}, u32[]{:S(2)}, u32[]{:S(2)}) collective-permute-start(bf16[256,3072]{0,1:T(8,128)(2,1)} %get-tuple-element.858), channel_id=1, source_target_pairs={{3,0},{4,1},{5,2},{6,3},{7,4},{11,8},{12,9},{13,10},{14,11},{15,12... | collective-permute-start | bytes 4718600 | tf_op jit(solution)/shard_map/ppermute | solution.py:14
  2541.1 3.8 collective-permute-start.11
  2545.8 62.1 %copy-start.20 = (bf16[1,256,1536]{2,1,0:T(8,128)(2,1)S(1)}, bf16[1,256,1536]{2,1,0:T(8,128)(2,1)}, u32[]{:S(2)}) copy-start(bf16[1,256,1536]{2,1,0:T(8,128)(2,1)} %param.18) | copy-start | bytes 2359300
  2545.8 62.1 %copy-start.30 = (bf16[251,8,2,96]{0,3,2,1:T(8,128)(2,1)S(1)}, bf16[251,8,2,96]{0,3,2,1:T(8,128)(2,1)}, u32[]{:S(2)}) copy-start(bf16[251,8,2,96]{0,3,2,1:T(8,128)(2,1)} %slice.3701) | copy-start | bytes 2313220
  2545.8 62.1 %copy-start.116 = (f32[1536]{0:T(1024)S(1)}, f32[1536]{0:T(1024)}, u32[]{:S(2)}) copy-start(f32[1536]{0:T(1024)} %param.25) | copy-start | bytes 18436
  2545.8 62.1 %copy-start.124 = (f32[256]{0:T(256)S(1)}, f32[256]{0:T(256)}, u32[]{:S(2)}) copy-start(f32[256]{0:T(256)} %copy-done.123) | copy-start | bytes 3076
  2617.0 335.9 %all-reduce.6.cloned.1.call-start = ((), (), s32[]{:S(2)}) async-start(), calls=%async_computation.11 | async-start | bytes 14155776 | tf_op jit(solution)/shard_map/psum | solution.py:356
  2617.1 15.9 slice-start
  2795.6 51.9 %copy-start.14 = (f32[256,1536]{1,0:T(8,128)S(1)}, f32[256,1536]{1,0:T(8,128)}, u32[]{:S(2)}) copy-start(f32[256,1536]{1,0:T(8,128)} %copy-done.13) | copy-start | bytes 4718596
  2795.6 51.9 %copy-start.135 = (f32[256]{0:T(256)S(1)}, f32[256]{0:T(256)}, u32[]{:S(2)}) copy-start(f32[256]{0:T(256)} %get-tuple-element.868) | copy-start | bytes 3076
  (764 other events, 5317.6 us)
Sparse Core Ops, SparseCore 0:
  9.7 132.3 all-gather.3
  143.7 75.9 all-gather.5
  221.9 99.1 all-gather.7
  839.9 83.2 reduce-scatter.6
  925.4 68.1 reduce-scatter.4
  1023.2 53.3 reduce-scatter.10
  2617.2 177.5 reduce-scatter.8
  2800.2 152.6 all-reduce.5
